TPU v7x, 512 devices: a whole 4x4x16 slice. The times are simulated.
512 devices in a mesh: dp: 8 (over z_hi, y), mp: 64 (over z_lo, x, core).
Axes of the slice: x: 4, y: 4, z: 16 (z_hi: 2, z_lo: 8; z = z_hi * 8 + z_lo), core: 2. Of those that a mesh axis runs over, the one named last changes fastest.
Arguments:
- tokens: bfloat16 [512, 6144], P(('dp', 'mp')), may hold values from -6 to 6
- w_in: bfloat16 [6144, 24576], P('dp', 'mp'), may hold values from -0.078125 to 0.078125
- w_out: bfloat16 [24576, 6144], P('mp', 'dp'), may hold values from -0.0390625 to 0.0390625
- cotangent: bfloat16 [512, 6144], P(('dp', 'mp')), may hold values from -6 to 6
Outputs:
- mixed: bfloat16 [512, 6144], P(('dp', 'mp'))
- grad_tokens: bfloat16 [512, 6144], P(('dp', 'mp'))
- grad_w_in: float32 [6144, 24576], P('dp', 'mp')
- grad_w_out: float32 [24576, 6144], P('mp', 'dp')
All inputs are finite; a program needn't handle non-finite values.
Results may differ from a plain program's by a relative error of at most 0.0054.
Values may be sent and summed in bfloat16 or wider, within the bound.
No kernel may reach another device: no remote copies, remote signals or barrier semaphores. Data moves between devices by JAX's collectives and lax.ppermute only.
A program may use at most 64 MiB of HBM per device.

v0:
```python
import jax
import jax.numpy as jnp
from jax import lax
from jax.sharding import PartitionSpec as P

epsilon = 1e-06


def gelu_tanh(values):
    return jax.nn.gelu(values, approximate=True)


def gelu_grad(pre_values, upstream):
    return jax.vjp(gelu_tanh, pre_values)[1](upstream)[0]


def spread(local_rows):
    row_count, feature_count = local_rows.shape
    groups = lax.axis_size("dp")
    width_block = feature_count // groups
    gathered = lax.all_gather(local_rows, "mp", axis=0, tiled=True)
    shaped = gathered.reshape(1, gathered.shape[0], groups, width_block)
    traded = lax.all_to_all(shaped, "dp", split_axis=2, concat_axis=0, tiled=True)
    return traded.reshape(groups * traded.shape[1], width_block)


def collect(partial_value, row_count):
    groups = lax.axis_size("dp")
    peer_count = lax.axis_size("mp")
    width_block = partial_value.shape[1]
    shaped = partial_value.reshape(groups, peer_count, row_count, width_block)
    summed = jnp.sum(lax.all_to_all(shaped, "mp", split_axis=1, concat_axis=1, tiled=True), axis=1)
    arrived = lax.all_to_all(summed, "dp", split_axis=0, concat_axis=2, tiled=True)
    return arrived.reshape(row_count, groups * width_block)


def group_total(term):
    return lax.psum(term, "dp")


def local(tokens, w_in, w_out, cotangent):
    contract_last = (((1,), (1,)), ((), ()))
    contract_first = (((0,), (0,)), ((), ()))
    tokens_wide = tokens.astype(jnp.float32)
    row_mean = jnp.mean(tokens_wide, axis=1, keepdims=True)
    centered = tokens_wide - row_mean
    inv_scale = lax.rsqrt(jnp.mean(centered * centered, axis=1, keepdims=True) + epsilon)
    unit_rows = centered * inv_scale
    normed = unit_rows.astype(jnp.bfloat16)
    row_count = tokens.shape[0]
    flat_normed = spread(normed)
    flat_grad = spread(cotangent)
    pre_all = group_total(jnp.dot(flat_normed, w_in, preferred_element_type=jnp.float32))
    act_all = gelu_tanh(pre_all).astype(jnp.bfloat16)
    branch_out = collect(jnp.dot(act_all, w_out, preferred_element_type=jnp.float32), row_count)
    mixed = (tokens_wide + branch_out).astype(jnp.bfloat16)
    act_grad = group_total(
        lax.dot_general(flat_grad, w_out, contract_last, preferred_element_type=jnp.float32)
    )
    pre_grad = gelu_grad(pre_all, act_grad).astype(jnp.bfloat16)
    grad_w_out = lax.dot_general(
        act_all, flat_grad, contract_first, preferred_element_type=jnp.float32
    )
    grad_w_in = lax.dot_general(
        flat_normed, pre_grad, contract_first, preferred_element_type=jnp.float32
    )
    normed_grad = collect(
        lax.dot_general(pre_grad, w_in, contract_last, preferred_element_type=jnp.float32),
        row_count,
    )
    row_inner = jnp.mean(normed_grad * unit_rows, axis=1, keepdims=True)
    through = inv_scale * (
        normed_grad - jnp.mean(normed_grad, axis=1, keepdims=True) - unit_rows * row_inner
    )
    grad_tokens = (cotangent.astype(jnp.float32) + through).astype(jnp.bfloat16)
    return (mixed, grad_tokens, grad_w_in, grad_w_out)


def solution(mesh):
    return jax.shard_map(
        local,
        mesh=mesh,
        in_specs=(P(("dp", "mp"), None), P("dp", "mp"), P("mp", "dp"), P(("dp", "mp"), None)),
        out_specs=(P(("dp", "mp"), None), P(("dp", "mp"), None), P("dp", "mp"), P("mp", "dp")),
        check_vma=False,
    )
```

profile of v0, /device:TPU:2, one launch (start us, length us, event | category | flops | bytes accessed | tf_op | source)
XLA Modules:
  0.0 757.5 jit_solution(10573223621665218163)
XLA Ops:
  7.2 1.5 convert_reduce_fusion
  9.3 1.4 multiply_reduce_fusion.1
  11.4 0.8 convert_bitcast_fusion
  12.2 123.8 %all-gather = bf16[64,1,6144]{2,1,0:T(2,128)(2,1)S(1)} all-gather(bf16[1,1,6144]{2,1,0:T(2,128)(2,1)S(1)} %convert_bitcast_fusion), channel_id=1, replica_groups=mesh['dp'=8,'mp'=64] {'mp'}, dimensions={0}, use_global_device_ids=true | all-gather | bytes 798720 | tf_op jit(solution)/shard_map/all_gather | solution.py:21
  135.9 4.7 reduce.7
  140.8 1.0 copy.10
  141.8 11.4 %all-to-all-start = ((bf16[1,64,8,768]{3,1,0,2:T(8,128)(2,1)}), bf16[1,64,8,768]{3,1,0,2:T(8,128)(2,1)S(1)}, u32[]{:S(2)}, u32[]{:S(2)}) async-start(bf16[1,64,8,768]{3,1,0,2:T(8,128)(2,1)} %copy.10), calls=%async_computation | async-start | bytes 1572864 | tf_op jit(solution)/shard_map/all_to_all | solution.py:23
  153.2 140.4 %all-gather.1 = bf16[64,1,6144]{2,1,0:T(2,128)(2,1)S(1)} all-gather(bf16[1,1,6144]{2,1,0:T(2,128)(2,1)S(1)} %bitcast.46), channel_id=1, replica_groups=mesh['dp'=8,'mp'=64] {'mp'}, dimensions={0}, use_global_device_ids=true | all-gather | bytes 798720 | tf_op jit(solution)/shard_map/all_gather | solution.py:21
  293.6 5.6 reduce.8
  299.2 1.3 copy.15
  300.5 1.0 copy.12
  301.5 13.5 %all-to-all-start.3 = ((bf16[1,64,8,768]{3,1,0,2:T(8,128)(2,1)}), bf16[1,64,8,768]{3,1,0,2:T(8,128)(2,1)S(1)}, u32[]{:S(2)}, u32[]{:S(2)}) async-start(bf16[1,64,8,768]{3,1,0,2:T(8,128)(2,1)} %copy.12), calls=%async_computation.3 | async-start | bytes 1572864 | tf_op jit(solution)/shard_map/all_to_all | solution.py:23
  315.0 1.5 fusion.10
  316.5 19.4 %all-to-all-done.3 = bf16[1,64,8,768]{3,1,0,2:T(8,128)(2,1)S(1)} async-done(((bf16[1,64,8,768]{3,1,0,2:T(8,128)(2,1)}), bf16[1,64,8,768]{3,1,0,2:T(8,128)(2,1)S(1)}, u32[]{:S(2)}, u32[]{:S(2)}) %all-to-all-start.3) | async-done | bytes 786464 | tf_op jit(solution)/shard_map/all_to_all | solution.py:23
  335.9 1.5 fusion.11
  337.4 195.6 %all-reduce.3.cloned.1.call-done = (f32[512,384]{1,0:T(8,128)}, f32[512,384]{1,0:T(8,128)}) async-done(((f32[512,384]{1,0:T(8,128)}, f32[512,384]{1,0:T(8,128)}), (f32[512,384]{1,0:T(8,128)}, f32[512,384]{1,0:T(8,128)})) %all-reduce.3.cloned.1.call-update) | async-done | bytes 1572880 | tf_op jit(solution)/shard_map/psum | solution.py:38
  533.0 1.9 fusion.6
  535.5 2.1 copy.13
  537.6 14.7 %all-to-all-start.4 = ((f32[8,64,1,768]{3,0,2,1:T(8,128)}), f32[8,64,1,768]{3,0,2,1:T(8,128)S(1)}, u32[]{:S(2)}, u32[]{:S(2)}) async-start(f32[8,64,1,768]{3,0,2,1:T(8,128)} %copy.13), calls=%async_computation.4 | async-start | bytes 3145728 | tf_op jit(solution)/shard_map/all_to_all | solution.py:32
  552.3 2.0 fusion.9
  554.3 2.1 copy.11
  556.3 69.7 %all-to-all-done.4 = f32[8,64,1,768]{3,0,2,1:T(8,128)S(1)} async-done(((f32[8,64,1,768]{3,0,2,1:T(8,128)}), f32[8,64,1,768]{3,0,2,1:T(8,128)S(1)}, u32[]{:S(2)}, u32[]{:S(2)}) %all-to-all-start.4) | async-done | bytes 1572896 | tf_op jit(solution)/shard_map/all_to_all | solution.py:32
  626.0 1.1 copy-done.1
  627.2 8.0 %all-to-all-start.1 = ((f32[8,64,1,768]{3,0,2,1:T(8,128)}), f32[8,64,1,768]{3,0,2,1:T(8,128)S(1)}, u32[]{:S(2)}, u32[]{:S(2)}) async-start(f32[8,64,1,768]{3,0,2,1:T(8,128)} %copy.11), calls=%async_computation.1 | async-start | bytes 3145728 | tf_op jit(solution)/shard_map/all_to_all | solution.py:32
  635.2 3.0 fusion.8
  638.2 1.5 reduce_sum.62
  640.3 68.6 %all-to-all-done.1 = f32[8,64,1,768]{3,0,2,1:T(8,128)S(1)} async-done(((f32[8,64,1,768]{3,0,2,1:T(8,128)}), f32[8,64,1,768]{3,0,2,1:T(8,128)S(1)}, u32[]{:S(2)}, u32[]{:S(2)}) %all-to-all-start.1) | async-done | bytes 1572896 | tf_op jit(solution)/shard_map/all_to_all | solution.py:32
  708.9 7.9 %all-to-all-start.5 = ((f32[8,1,768]{2,1,0:T(1,128)}), f32[8,1,768]{2,1,0:T(1,128)S(1)}, u32[]{:S(2)}, u32[]{:S(2)}) async-start(f32[8,1,768]{2,1,0:T(1,128)} %reduce_sum.63), calls=%async_computation.5 | async-start | bytes 49152 | tf_op jit(solution)/shard_map/all_to_all | solution.py:33
  716.8 1.6 fusion.13
  719.2 12.6 %all-to-all-done.5 = f32[8,1,768]{2,1,0:T(1,128)S(1)} async-done(((f32[8,1,768]{2,1,0:T(1,128)}), f32[8,1,768]{2,1,0:T(1,128)S(1)}, u32[]{:S(2)}, u32[]{:S(2)}) %all-to-all-start.5) | async-done | bytes 24608 | tf_op jit(solution)/shard_map/all_to_all | solution.py:33
  731.8 3.3 all-to-all-start.2
  737.7 12.3 %all-to-all-done.2 = f32[8,1,768]{2,1,0:T(1,128)S(1)} async-done(((f32[8,1,768]{2,1,0:T(1,128)}), f32[8,1,768]{2,1,0:T(1,128)S(1)}, u32[]{:S(2)}, u32[]{:S(2)}) %all-to-all-start.2) | async-done | bytes 24608 | tf_op jit(solution)/shard_map/all_to_all | solution.py:33
  (22 shorter events, 4.2 us)
Async XLA Ops:
  7.2 307.9 %copy-start = (bf16[768,384]{1,0:T(8,128)(2,1)S(1)}, bf16[768,384]{1,0:T(8,128)(2,1)}, u32[]{:S(2)}) copy-start(bf16[768,384]{1,0:T(8,128)(2,1)} %param.5) | copy-start | bytes 1769476
  140.8 12.4 %copy-start.5 = (bf16[1,6144]{1,0:T(2,128)(2,1)S(1)}, bf16[1,6144]{1,0:T(2,128)(2,1)}, u32[]{:S(2)}) copy-start(bf16[1,6144]{1,0:T(2,128)(2,1)} %param.7) | copy-start | bytes 36868
  141.8 159.7 %all-to-all-start = ((bf16[1,64,8,768]{3,1,0,2:T(8,128)(2,1)}), bf16[1,64,8,768]{3,1,0,2:T(8,128)(2,1)S(1)}, u32[]{:S(2)}, u32[]{:S(2)}) async-start(bf16[1,64,8,768]{3,1,0,2:T(8,128)(2,1)} %copy.10), calls=%async_computation | async-start | bytes 1572864 | tf_op jit(solution)/shard_map/all_to_all | solution.py:23
  301.5 34.4 %copy-start.3 = (bf16[384,768]{1,0:T(8,128)(2,1)S(1)}, bf16[384,768]{1,0:T(8,128)(2,1)}, u32[]{:S(2)}) copy-start(bf16[384,768]{1,0:T(8,128)(2,1)} %param.6) | copy-start | bytes 1769476
  301.5 34.4 %all-to-all-start.3 = ((bf16[1,64,8,768]{3,1,0,2:T(8,128)(2,1)}), bf16[1,64,8,768]{3,1,0,2:T(8,128)(2,1)S(1)}, u32[]{:S(2)}, u32[]{:S(2)}) async-start(bf16[1,64,8,768]{3,1,0,2:T(8,128)(2,1)} %copy.12), calls=%async_computation.3 | async-start | bytes 1572864 | tf_op jit(solution)/shard_map/all_to_all | solution.py:23
  315.0 218.0 %all-reduce.3.cloned.1.call-start = ((), (), s32[]{:S(2)}) async-start(), calls=%async_computation.6 | async-start | bytes 3145728 | tf_op jit(solution)/shard_map/psum | solution.py:38
  335.9 1.5 copy-start.2
  537.6 88.4 %all-to-all-start.4 = ((f32[8,64,1,768]{3,0,2,1:T(8,128)}), f32[8,64,1,768]{3,0,2,1:T(8,128)S(1)}, u32[]{:S(2)}, u32[]{:S(2)}) async-start(f32[8,64,1,768]{3,0,2,1:T(8,128)} %copy.13), calls=%async_computation.4 | async-start | bytes 3145728 | tf_op jit(solution)/shard_map/all_to_all | solution.py:32
  626.0 1.1 copy-start.1
  627.2 81.8 %all-to-all-start.1 = ((f32[8,64,1,768]{3,0,2,1:T(8,128)}), f32[8,64,1,768]{3,0,2,1:T(8,128)S(1)}, u32[]{:S(2)}, u32[]{:S(2)}) async-start(f32[8,64,1,768]{3,0,2,1:T(8,128)} %copy.11), calls=%async_computation.1 | async-start | bytes 3145728 | tf_op jit(solution)/shard_map/all_to_all | solution.py:32
  708.9 22.8 %all-to-all-start.5 = ((f32[8,1,768]{2,1,0:T(1,128)}), f32[8,1,768]{2,1,0:T(1,128)S(1)}, u32[]{:S(2)}, u32[]{:S(2)}) async-start(f32[8,1,768]{2,1,0:T(1,128)} %reduce_sum.63), calls=%async_computation.5 | async-start | bytes 49152 | tf_op jit(solution)/shard_map/all_to_all | solution.py:33
  716.8 19.6 %copy-start.4 = (bf16[1,6144]{1,0:T(2,128)(2,1)S(1)}, bf16[1,6144]{1,0:T(2,128)(2,1)}, u32[]{:S(2)}) copy-start(bf16[1,6144]{1,0:T(2,128)(2,1)} %param.4) | copy-start | bytes 36868
  731.8 18.2 %all-to-all-start.2 = ((f32[8,1,768]{2,1,0:T(1,128)}), f32[8,1,768]{2,1,0:T(1,128)S(1)}, u32[]{:S(2)}, u32[]{:S(2)}) async-start(f32[8,1,768]{2,1,0:T(1,128)} %reduce_sum.61), calls=%async_computation.2 | async-start | bytes 49152 | tf_op jit(solution)/shard_map/all_to_all | solution.py:33
Sparse Core Ops, SparseCore 0:
  337.5 195.4 all-reduce.2
where the time goes:
time: 758 us
  waiting for transfers between devices  378 us (50%)
  blocking collectives  264 us (35%)
  starting transfers between devices  58.8 us (8%)
  other arithmetic  19.5 us (3%)
  between operations  16.8 us (2%)
  matrix products  10.1 us (1%)
  local copies, waits for them, and re-layouts  10 us (1%)
    all_gather x2, blocking collectives, spread(): gathered = lax.all_gather(local_rows, 'mp', axis=0, tiled=True)  264 us
    psum x1, waiting for transfers between devices, group_total(): return lax.psum(term, 'dp')  196 us
    all_to_all x2, waiting for transfers between devices, collect(): lax.all_to_all(shaped, 'mp', split_axis=1, concat_axis=1, tiled=True)  138 us
    all_to_all x2, starting transfers between devices, spread(): lax.all_to_all(shaped, 'dp', split_axis=2, concat_axis=0, tiled=True)  24.9 us
    all_to_all x2, waiting for transfers between devices, collect(): lax.all_to_all(summed, 'dp', split_axis=0, concat_axis=2, tiled=True)  24.9 us
    all_to_all x2, starting transfers between devices, collect(): lax.all_to_all(shaped, 'mp', split_axis=1, concat_axis=1, tiled=True)  22.7 us
    all_to_all x2, waiting for transfers between devices, spread(): lax.all_to_all(shaped, 'dp', split_axis=2, concat_axis=0, tiled=True)  19.4 us
  transfers between devices with their start and end apart: 7, of which 6 were waited for; matrix products, arithmetic and copies ran while one was open for 3% of the time, Pallas kernels for 0%

commit v1 on v0

--- a/solution.py
+++ b/solution.py
@@ -35,7 +35,7 @@
 
 
 def group_total(term):
-    return lax.psum(term, "dp")
+    return jnp.sum(lax.all_gather(term, "dp"), axis=0)
 
 
 def local(tokens, w_in, w_out, cotangent):

time: 758 us -> 921 us (1.22)
  blocking collectives: 264 us -> 398 us
  waiting for transfers between devices: 378 us -> 413 us
  starting transfers between devices: 58.8 us -> 49 us
    all_gather x0 -> x2, waiting for transfers between devices: none -> 250 us  [group_total(): return jnp.sum(lax.all_gather(term, 'dp'), axis=0)]
    psum x1 -> x0, waiting for transfers between devices: 196 us -> none  [group_total(): return lax.psum(term, 'dp')]
    all_to_all x0 -> x2, blocking collectives: none -> 72.4 us  [spread(): lax.all_to_all(shaped, 'dp', split_axis=2, concat_axis=0, tiled=True)]
    all_gather x2, blocking collectives: 264 us -> 325 us  [spread(): gathered = lax.all_gather(local_rows, 'mp', axis=0, tiled=True)]
    all_to_all x2 -> x0, starting transfers between devices: 24.9 us -> none  [spread(): lax.all_to_all(shaped, 'dp', split_axis=2, concat_axis=0, tiled=True)]
    all_to_all x2 -> x0, waiting for transfers between devices: 19.4 us -> none  [spread(): lax.all_to_all(shaped, 'dp', split_axis=2, concat_axis=0, tiled=True)]
    all_to_all x2, starting transfers between devices: 22.7 us -> 37.2 us  [collect(): lax.all_to_all(shaped, 'mp', split_axis=1, concat_axis=1, tiled=True)]
  transfers between devices with their start and end apart: 7 -> 6, of which waited for: 6 -> 5; matrix products, arithmetic and copies ran while one was open for 3% -> 3% of each run, Pallas kernels for 0% -> 0%
where the time goes in v1:
time: 921 us; the launch traced here: 920 us
  waiting for transfers between devices  413 us (45%)
  blocking collectives  398 us (43%)
  starting transfers between devices  49 us (5%)
  other arithmetic  27.9 us (3%)
  between operations  16.8 us (2%)
    all_gather x2, blocking collectives, spread(): gathered = lax.all_gather(local_rows, 'mp', axis=0, tiled=True)  325 us
    all_gather x2, waiting for transfers between devices, group_total(): return jnp.sum(lax.all_gather(term, 'dp'), axis=0)  250 us
    all_to_all x2, waiting for transfers between devices, collect(): lax.all_to_all(shaped, 'mp', split_axis=1, concat_axis=1, tiled=True)  140 us
    all_to_all x2, blocking collectives, spread(): lax.all_to_all(shaped, 'dp', split_axis=2, concat_axis=0, tiled=True)  72.4 us
    all_to_all x2, starting transfers between devices, collect(): lax.all_to_all(shaped, 'mp', split_axis=1, concat_axis=1, tiled=True)  37.2 us
    all_to_all x2, waiting for transfers between devices, collect(): lax.all_to_all(summed, 'dp', split_axis=0, concat_axis=2, tiled=True)  23.4 us
  transfers between devices with their start and end apart: 6, of which 5 were waited for; matrix products, arithmetic and copies ran while one was open for 3% of the time, Pallas kernels for 0%

profile of v1, /device:TPU:2, one launch (start us, length us, event | category | flops | bytes accessed | tf_op | source)
XLA Modules:
  0.0 920.3 jit_solution(292134303519451277)
XLA Ops:
  7.2 1.4 convert_reduce_fusion
  9.3 1.4 multiply_reduce_fusion.1
  11.4 0.8 convert_bitcast_fusion
  12.2 122.7 %all-gather.2 = bf16[64,1,6144]{2,1,0:T(2,128)(2,1)S(1)} all-gather(bf16[1,1,6144]{2,1,0:T(2,128)(2,1)S(1)} %convert_bitcast_fusion), channel_id=1, replica_groups=mesh['dp'=8,'mp'=64] {'mp'}, dimensions={0}, use_global_device_ids=true | all-gather | bytes 798720 | tf_op jit(solution)/shard_map/all_gather | solution.py:21
  134.9 4.7 reduce.7
  139.9 34.1 %all_to_all.58 = bf16[1,64,8,768]{3,1,0,2:T(8,128)(2,1)S(1)} all-to-all(bf16[1,64,8,768]{3,1,0,2:T(8,128)(2,1)S(1)} %copy.10), channel_id=1, replica_groups=mesh['dp'=8,'mp'=64] {'dp'}, dimensions={2} | all-to-all | bytes 1572864 | tf_op jit(solution)/shard_map/all_to_all | solution.py:23
  174.0 1.5 fusion.10
  175.5 202.8 %all-gather.3 = bf16[64,1,6144]{2,1,0:T(2,128)(2,1)S(1)} all-gather(bf16[1,1,6144]{2,1,0:T(2,128)(2,1)S(1)} %bitcast.50), channel_id=1, replica_groups=mesh['dp'=8,'mp'=64] {'mp'}, dimensions={0}, use_global_device_ids=true | all-gather | bytes 798720 | tf_op jit(solution)/shard_map/all_gather | solution.py:21
  378.3 5.6 reduce.8
  383.9 1.4 copy.15
  385.4 38.4 %all_to_all.59 = bf16[1,64,8,768]{3,1,0,2:T(8,128)(2,1)S(1)} all-to-all(bf16[1,64,8,768]{3,1,0,2:T(8,128)(2,1)S(1)} %copy.12), channel_id=1, replica_groups=mesh['dp'=8,'mp'=64] {'dp'}, dimensions={2} | all-to-all | bytes 1572864 | tf_op jit(solution)/shard_map/all_to_all | solution.py:23
  423.8 1.5 fusion.11
  425.3 3.2 reduce_sum.78
  428.5 249.7 %all-gather.9.cloned.1.call-done = f32[4096,384]{1,0:T(8,128)} async-done(((f32[512,384]{1,0:T(8,128)}), f32[4096,384]{1,0:T(8,128)}) %all-gather.9.cloned.1.call-update) | async-done | bytes 6291472 | tf_op jit(solution)/shard_map/all_gather | solution.py:38
  678.2 4.0 reduce_sum.81
  682.3 1.7 fusion.6
  684.5 2.1 copy.13
  686.6 28.8 %all-to-all-start.4 = ((f32[8,64,1,768]{3,0,2,1:T(8,128)}), f32[8,64,1,768]{3,0,2,1:T(8,128)}, u32[]{:S(2)}, u32[]{:S(2)}) async-start(f32[8,64,1,768]{3,0,2,1:T(8,128)} %copy.13), calls=%async_computation.4 | async-start | bytes 3145728 | tf_op jit(solution)/shard_map/all_to_all | solution.py:32
  715.3 1.7 fusion.9
  717.1 2.1 copy.11
  719.1 69.9 %all-to-all-done.4 = f32[8,64,1,768]{3,0,2,1:T(8,128)} async-done(((f32[8,64,1,768]{3,0,2,1:T(8,128)}), f32[8,64,1,768]{3,0,2,1:T(8,128)}, u32[]{:S(2)}, u32[]{:S(2)}) %all-to-all-start.4) | async-done | bytes 1572896 | tf_op jit(solution)/shard_map/all_to_all | solution.py:32
  789.0 8.4 all-to-all-start.1
  797.4 1.6 fusion.8
  799.0 1.5 reduce_sum.82
  801.2 69.9 %all-to-all-done.1 = f32[8,64,1,768]{3,0,2,1:T(8,128)} async-done(((f32[8,64,1,768]{3,0,2,1:T(8,128)}), f32[8,64,1,768]{3,0,2,1:T(8,128)}, u32[]{:S(2)}, u32[]{:S(2)}) %all-to-all-start.1) | async-done | bytes 1572896 | tf_op jit(solution)/shard_map/all_to_all | solution.py:32
  871.1 8.5 all-to-all-start.5
  879.6 1.6 fusion.13
  881.2 1.5 reduce_sum.79
  883.3 11.2 %all-to-all-done.5 = f32[8,1,768]{2,1,0:T(1,128)S(1)} async-done(((f32[8,1,768]{2,1,0:T(1,128)}), f32[8,1,768]{2,1,0:T(1,128)S(1)}, u32[]{:S(2)}, u32[]{:S(2)}) %all-to-all-start.5) | async-done | bytes 24608 | tf_op jit(solution)/shard_map/all_to_all | solution.py:33
  894.5 3.3 all-to-all-start.2
  900.5 12.3 %all-to-all-done.2 = f32[8,1,768]{2,1,0:T(1,128)S(1)} async-done(((f32[8,1,768]{2,1,0:T(1,128)}), f32[8,1,768]{2,1,0:T(1,128)S(1)}, u32[]{:S(2)}, u32[]{:S(2)}) %all-to-all-start.2) | async-done | bytes 24608 | tf_op jit(solution)/shard_map/all_to_all | solution.py:33
  912.8 0.7 add_convert_fusion
  (21 shorter events, 3.7 us)
Async XLA Ops:
  7.2 166.8 %copy-start = (bf16[768,384]{1,0:T(8,128)(2,1)S(1)}, bf16[768,384]{1,0:T(8,128)(2,1)}, u32[]{:S(2)}) copy-start(bf16[768,384]{1,0:T(8,128)(2,1)} %param.5) | copy-start | bytes 1769476
  7.2 418.1 %all-gather.7.cloned.1.call-start = ((), (), s32[]{:S(2)}) async-start(), calls=%async_computation.6 | async-start | bytes 7077888 | tf_op jit(solution)/shard_map/all_gather | solution.py:38
  174.0 1.5 copy-start.3
  175.4 502.8 %all-gather.9.cloned.1.call-start = ((), (), s32[]{:S(2)}) async-start(), calls=%async_computation.7 | async-start | bytes 7077888 | tf_op jit(solution)/shard_map/all_gather | solution.py:38
  385.3 38.5 %copy-start.1 = (bf16[384,768]{1,0:T(8,128)(2,1)S(1)}, bf16[384,768]{1,0:T(8,128)(2,1)}, u32[]{:S(2)}) copy-start(bf16[384,768]{1,0:T(8,128)(2,1)} %param.6) | copy-start | bytes 1769476
  686.6 102.4 %all-to-all-start.4 = ((f32[8,64,1,768]{3,0,2,1:T(8,128)}), f32[8,64,1,768]{3,0,2,1:T(8,128)}, u32[]{:S(2)}, u32[]{:S(2)}) async-start(f32[8,64,1,768]{3,0,2,1:T(8,128)} %copy.13), calls=%async_computation.4 | async-start | bytes 3145728 | tf_op jit(solution)/shard_map/all_to_all | solution.py:32
  789.0 82.1 %all-to-all-start.1 = ((f32[8,64,1,768]{3,0,2,1:T(8,128)}), f32[8,64,1,768]{3,0,2,1:T(8,128)}, u32[]{:S(2)}, u32[]{:S(2)}) async-start(f32[8,64,1,768]{3,0,2,1:T(8,128)} %copy.11), calls=%async_computation.1 | async-start | bytes 3145728 | tf_op jit(solution)/shard_map/all_to_all | solution.py:32
  871.1 23.4 %all-to-all-start.5 = ((f32[8,1,768]{2,1,0:T(1,128)}), f32[8,1,768]{2,1,0:T(1,128)S(1)}, u32[]{:S(2)}, u32[]{:S(2)}) async-start(f32[8,1,768]{2,1,0:T(1,128)} %reduce_sum.83), calls=%async_computation.5 | async-start | bytes 49152 | tf_op jit(solution)/shard_map/all_to_all | solution.py:33
  879.6 18.3 %copy-start.2 = (bf16[1,6144]{1,0:T(2,128)(2,1)S(1)}, bf16[1,6144]{1,0:T(2,128)(2,1)}, u32[]{:S(2)}) copy-start(bf16[1,6144]{1,0:T(2,128)(2,1)} %param.4) | copy-start | bytes 36868
  894.5 18.2 %all-to-all-start.2 = ((f32[8,1,768]{2,1,0:T(1,128)}), f32[8,1,768]{2,1,0:T(1,128)S(1)}, u32[]{:S(2)}, u32[]{:S(2)}) async-start(f32[8,1,768]{2,1,0:T(1,128)} %reduce_sum.80), calls=%async_computation.2 | async-start | bytes 49152 | tf_op jit(solution)/shard_map/all_to_all | solution.py:33
Sparse Core Ops, SparseCore 0:
  175.6 226.2 all-gather.6
  425.4 252.7 all-gather.8
